TPU v7x, 768 devices: a whole 4x8x12 slice. The times are simulated.
768 devices in a mesh: lat: 16 (over z_hi, x), lon: 48 (over z_lo, y, core).
Axes of the slice: x: 4, y: 8, z: 12 (z_hi: 4, z_lo: 3; z = z_hi * 3 + z_lo), core: 2. Of those that a mesh axis runs over, the one named last changes fastest.
Arguments:
- ensemble: bfloat16 [192, 128, 10240], P('lon', 'lat'), may hold values from -0.625 to 0.625
- innovation: float32 [384, 256, 128], P('lon', 'lat'), may hold values from -6 to 6
- obs_weight: float32 [384, 256, 128], P('lon', 'lat'), may hold values from 0.5 to 20
- lat_offset: int32 [256], P('lat'), may hold values from 0 to 3
- lat_weight: float32 [256], P('lat'), may hold values from 0 to 1
- band_widths: int32 [80], replicated, may hold values from 1 to 63
Outputs:
- coefficients: float32 [2, 2], replicated
- next_vector: bfloat16 [192, 128, 5120], P('lon', 'lat')
All inputs are finite; a program needn't handle non-finite values.
Results may differ from a plain program's by a relative error of at most 0.0014.
Values sent between devices are 32-bit elements; how exact they have to be, the bound alone decides.
A program may use at most 32 MiB of HBM per device.

v0:
```python
import functools

import jax
import jax.numpy as jnp
from jax import lax
from jax.experimental import pallas as pl
from jax.experimental.pallas import tpu as pltpu
from jax.sharding import PartitionSpec as P

M = 80
LEV = 64
PAIRS = M // 2
EVEN_TAPS = (-0.0234375, 0.2265625, 0.8671875, -0.0703125)
ODD_TAPS = (-0.0703125, 0.8671875, 0.2265625, -0.0234375)
EPSILON = 1e-06
F32 = jnp.float32
BF16 = jnp.bfloat16
MESH = pl.DeviceIdType.MESH
TOPO = (4, 4, 3, 8, 2)
DIRECTIONS = ((1, 1), (1, -1), (-1, 1), (-1, -1), (1, 0), (-1, 0), (0, 1), (0, -1))
UNROLL = 4


def kernel(
    topo,
    entries,
    ens_hbm,
    innov_hbm,
    wobs_hbm,
    offset_ref,
    weight_ref,
    bands_ref,
    coef_out,
    vec_out,
    ens,
    dext,
    wext,
    wsplit,
    zext,
    yv,
    params,
    coef,
    gbuf,
    tents,
    sq_hi,
    sq_lo,
    inv2,
    uvec,
    red_a,
    red_b,
    red_c,
    local_sem,
    in_send,
    in_recv,
    par_send,
    par_recv,
    z_send,
    z_recv,
    a_send,
    a_recv,
    b_send,
    b_recv,
    c_send,
    c_recv,
):
    zh_n, x_n, zl_n, y_n, core_n = topo
    lat_n, lon_n = zh_n * x_n, zl_n * y_n * core_n
    lat, lon = lax.axis_index("lat"), lax.axis_index("lon")
    z_hi, x = lat // x_n, lat % x_n
    z_lo, y_core = lon // (y_n * core_n), lon % (y_n * core_n)
    y_pos, core = y_core // core_n, y_core % core_n

    def neighbour(dlat, dlon):
        return (lat + dlat, lax.rem(lon + dlon + lon_n, lon_n))

    def inside(dlat, body):
        if dlat == 0:
            body()
        else:
            pl.when((lat + dlat >= 0) & (lat + dlat < lat_n))(body)

    def dev_a(i):
        return (z_hi * x_n + i // core_n, lon - core + i % core_n)

    def dev_b(i):
        return (lat, z_lo * (y_n * core_n) + i * core_n + core)

    def dev_c(i):
        return ((i // zl_n) * x_n + x, (i % zl_n) * (y_n * core_n) + y_core)

    stages = (
        (x * core_n + core, x_n * core_n, dev_a, red_a, a_send, a_recv),
        (y_pos, y_n, dev_b, red_b, b_send, b_recv),
        (z_hi * zl_n + z_lo, zh_n * zl_n, dev_c, red_c, c_send, c_recv),
    )

    dext[...] = jnp.zeros(dext.shape, F32)
    wext[...] = jnp.zeros(wext.shape, F32)
    zext[...] = jnp.zeros(zext.shape, F32)
    params[...] = jnp.zeros(params.shape, F32)
    params[1, 0:1, 0:16] = weight_ref[...]
    params[1, 1:2, 0:16] = offset_ref[...].astype(F32)

    barrier = pltpu.get_barrier_semaphore()
    for dlat, dlon in DIRECTIONS:

        def greet(dlat=dlat, dlon=dlon):
            pl.semaphore_signal(
                barrier, inc=1, device_id=neighbour(dlat, dlon), device_id_type=MESH
            )

        inside(dlat, greet)
    for me, count, device, _, _, _ in stages:
        for step in range(1, count):
            pl.semaphore_signal(
                barrier,
                inc=1,
                device_id=device(lax.rem(me + step, count)),
                device_id_type=MESH,
            )

    own_d = pltpu.make_async_copy(innov_hbm, dext.at[3:11, 8:24], local_sem.at[0])
    own_w = pltpu.make_async_copy(wobs_hbm, wext.at[3:11, 8:24], local_sem.at[1])
    own_e = pltpu.make_async_copy(ens_hbm, ens, local_sem.at[2])
    own_d.start()
    own_w.start()
    own_e.start()

    rows = lax.broadcasted_iota(jnp.int32, (128, 128), 0)
    cols = lax.broadcasted_iota(jnp.int32, (128, 128), 1)
    same = (rows < LEV) == (cols < LEV)
    distance = jnp.where(same, jnp.abs(rows - cols), 1000)
    first_half = lax.broadcasted_iota(jnp.int32, (1, 128), 1) < LEV

    def build(j, carry):
        width = jnp.where(first_half, bands_ref[2 * j] + 1, bands_ref[2 * j + 1] + 1)
        tent = jnp.maximum(width - distance, 0).astype(F32).astype(BF16)
        wide = width.astype(F32)
        scale = 1.0 / (wide * wide)
        square = jnp.dot(tent, tent, preferred_element_type=F32) * (scale * scale)
        high = square.astype(BF16)
        tents[j] = tent
        sq_hi[j] = high
        sq_lo[j] = (square - high.astype(F32)).astype(BF16)
        inv2[j] = jnp.broadcast_to(scale, (8, 128))
        return carry

    lax.fori_loop(0, PAIRS, build, 0)

    edges = (lat == 0).astype(jnp.int32) + (lat == lat_n - 1).astype(jnp.int32)
    others = sum(count - 1 for _, count, _, _, _, _ in stages)
    pl.semaphore_wait(barrier, others + 8 - 3 * edges)

    def cut(delta, size, width, before):
        if delta == 0:
            return slice(0, size), slice(before, before + size)
        if delta == 1:
            return slice(size - width, size), slice(before - width, before)
        return slice(0, width), slice(before + size, before + size + width)

    def input_copies(which, dlat, dlon):
        src_cols, dst_cols = cut(dlon, 8, 3, 3)
        src_rows, dst_rows = cut(dlat, 16, 8, 8)
        number = DIRECTIONS.index((dlat, dlon))
        pairs = ((innov_hbm, dext), (wobs_hbm, wext))
        src, dst = pairs[which]
        return pltpu.make_async_remote_copy(
            src_ref=src.at[src_cols, src_rows],
            dst_ref=dst.at[dst_cols, dst_rows],
            send_sem=in_send.at[which, number],
            recv_sem=in_recv.at[which, number],
            device_id=neighbour(dlat, dlon),
            device_id_type=MESH,
        )

    def param_copy(dlat):
        return pltpu.make_async_remote_copy(
            src_ref=params.at[1],
            dst_ref=params.at[1 - dlat],
            send_sem=par_send.at[(dlat + 1) // 2],
            recv_sem=par_recv.at[(dlat + 1) // 2],
            device_id=neighbour(dlat, 0),
            device_id_type=MESH,
        )

    def z_copy(phase, dlat, dlon):
        src_cols, dst_cols = cut(dlon, 4, 3, 3)
        src_rows, dst_rows = cut(dlat, 8, 8, 8)
        number = DIRECTIONS.index((dlat, dlon))
        src_cols = slice(src_cols.start + 3, src_cols.stop + 3)
        src_rows = slice(src_rows.start + 8, src_rows.stop + 8)
        return pltpu.make_async_remote_copy(
            src_ref=zext.at[phase, src_cols, src_rows],
            dst_ref=zext.at[phase, dst_cols, dst_rows],
            send_sem=z_send.at[phase, number],
            recv_sem=z_recv.at[phase, number],
            device_id=neighbour(dlat, dlon),
            device_id_type=MESH,
        )

    for dlat, dlon in DIRECTIONS:

        def send(dlat=dlat, dlon=dlon):
            input_copies(0, dlat, dlon).start()
            input_copies(1, dlat, dlon).start()
            if dlon == 0:
                param_copy(dlat).start()

        inside(dlat, send)

    own_d.wait()
    own_w.wait()
    own_e.wait()
    for dlat, dlon in DIRECTIONS:

        def receive(dlat=dlat, dlon=dlon):
            input_copies(0, dlat, dlon).wait_recv()
            input_copies(1, dlat, dlon).wait_recv()
            if dlon == 0:
                param_copy(dlat).wait_recv()

        inside(-dlat, receive)

    row = lax.broadcasted_iota(jnp.int32, (16, 128), 0)
    lane = lax.broadcasted_iota(jnp.int32, (16, 128), 1)
    for parity in range(2):
        fine = 2 * row - 4 + parity
        picked = []
        for kind in range(2):
            total = jnp.zeros((16, 128), F32)
            for source in range(3):
                line = jnp.broadcast_to(params[source, kind : kind + 1, :], (16, 128))
                total = total + jnp.where(lane == fine + 16 - 16 * source, line, 0.0)
            picked.append(
                jnp.broadcast_to(jnp.sum(total, axis=1, keepdims=True), (16, 128))
            )
        upper, offset = picked
        for k in range(5):
            coef[parity, k] = jnp.where(offset == float(k), 1.0 - upper, 0.0) + jnp.where(
                offset == float(k - 1), upper, 0.0
            )

    def restrict(fields):
        for parity in range(2):
            odd, even = fields(parity)
            total = jnp.zeros((4, 16, 128), F32)
            for t in range(4):
                total = total + ODD_TAPS[t] * odd[3 - t : 7 - t] + EVEN_TAPS[t] * even[3 - t : 7 - t]
            gbuf[parity] = total
        result = jnp.zeros((4, 8, 128), F32)
        for parity in range(2):
            for k in range(5):
                result = result + (
                    coef[parity, k, 4 - k : 12 - k, :][None] * gbuf[parity, :, 4 - k : 12 - k, :]
                )
        return result

    def start_field(parity):
        found = []
        for kind in range(2):
            column = []
            for b in range(7):
                at = pl.ds(4 + parity, 16, stride=2)
                weight = wext[2 * b + kind, at, :]
                wsplit[parity, kind, b] = weight
                column.append(weight * dext[2 * b + kind, at, :])
            found.append(jnp.stack(column))
        return found

    def fine_field(phase):
        def field(parity):
            along = jnp.zeros((10, 16, 128), F32)
            for k in range(5):
                along = along + coef[parity, k][None] * zext[phase, :, 4 + k : 20 + k, :]
            found = []
            for kind, taps in enumerate((ODD_TAPS, EVEN_TAPS)):
                total = taps[0] * along[0:7]
                for t in range(1, 4):
                    total = total + taps[t] * along[t : t + 7]
                found.append(wsplit[parity, kind] * total)
            return found

        return field

    first_lanes = lax.broadcasted_iota(jnp.int32, (4, 8, 128), 2) < LEV

    def split_pair(j, y):
        at = pl.multiple_of(j * 256, 256)
        e0 = ens[:, :, pl.ds(at, 128)].astype(F32)
        e1 = ens[:, :, pl.ds(at + 128, 128)].astype(F32)
        p0, p1 = e0 * y, e1 * y
        kept = jnp.where(first_lanes, p0, p1)
        moved = jnp.where(first_lanes, p1, p0)
        total = (kept + pltpu.roll(moved, LEV, 2)).reshape(32, 128)
        high = total.astype(BF16)
        low = (total - high.astype(F32)).astype(BF16)
        return e0, e1, high, low

    def combine_spread(y):
        def body(step, acc):
            for extra in range(UNROLL):
                j = step * UNROLL + extra
                e0, e1, high, low = split_pair(j, y)
                both = jnp.concatenate([high, low], axis=0)
                main = jnp.dot(both, sq_hi[j], preferred_element_type=F32)
                rest = jnp.dot(high, sq_lo[j], preferred_element_type=F32)
                out = (main[:32] + (main[32:] + rest)).reshape(4, 8, 128)
                turned = pltpu.roll(out, LEV, 2)
                acc = acc + e0 * jnp.where(first_lanes, out, turned)
                acc = acc + e1 * jnp.where(first_lanes, turned, out)
            return acc

        return lax.fori_loop(0, PAIRS // UNROLL, body, jnp.zeros((4, 8, 128), F32))

    def spread(which):
        y = yv[which]

        def body(step, carry):
            for extra in range(UNROLL):
                j = step * UNROLL + extra
                _, _, high, low = split_pair(j, y)
                both = jnp.concatenate([high, low], axis=0)
                main = jnp.dot(both, tents[j], preferred_element_type=F32)
                out = (main[:32] + main[32:]).reshape(4, 8, 128) * inv2[j][None]
                uvec[which, :, :, pl.ds(pl.multiple_of(j * 128, 128), 128)] = out
            return carry

        lax.fori_loop(0, PAIRS // UNROLL, body, 0)

    yv[0] = restrict(start_field)

    for phase in range(2):
        z = combine_spread(yv[phase])
        zext[phase, 3:7, 8:16, :] = z
        for dlat, dlon in DIRECTIONS:

            def send(dlat=dlat, dlon=dlon, phase=phase):
                z_copy(phase, dlat, dlon).start()

            inside(dlat, send)
        spread(phase)
        for dlat, dlon in DIRECTIONS:

            def receive(dlat=dlat, dlon=dlon, phase=phase):
                z_copy(phase, dlat, dlon).wait_recv()

            inside(-dlat, receive)
        yv[phase + 1] = restrict(fine_field(phase))

    z0, z1 = zext[0, 3:7, 8:16, :], zext[1, 3:7, 8:16, :]
    y0, y1, y2 = yv[0], yv[1], yv[2]
    lane1 = lax.broadcasted_iota(jnp.int32, (1, 128), 1)
    local = jnp.zeros((1, 128), F32)
    for number, (left, right) in enumerate(
        ((z0, y0), (z0, y1), (z1, y1), (z0, y2), (z1, y2))
    ):
        plane = jnp.sum(left * right, axis=0)
        value = jnp.sum(jnp.sum(plane, axis=0, keepdims=True), axis=1, keepdims=True)
        local = local + jnp.where(lane1 == number, jnp.broadcast_to(value, (1, 128)), 0.0)

    for number, (me, count, device, slots, send_sems, recv_sems) in enumerate(stages):

        def stage_copy(target, slot):
            return pltpu.make_async_remote_copy(
                src_ref=slots.at[me],
                dst_ref=slots.at[slot],
                send_sem=send_sems.at[target],
                recv_sem=recv_sems.at[slot],
                device_id=device(target),
                device_id_type=MESH,
            )

        slots[me] = local
        for step in range(1, count):
            stage_copy(lax.rem(me + step, count), me).start()
        if number == 0:
            spread(2)
        for step in range(1, count):
            other = lax.rem(me + step, count)
            stage_copy(other, other).wait_recv()
        local = slots[0]
        for slot in range(1, count):
            local = local + slots[slot]

    def picked(number):
        one = jnp.sum(jnp.where(lane1 == number, local, 0.0), axis=1, keepdims=True)
        return jnp.broadcast_to(one, (8, 128))

    a, b, d, e, f = (picked(number) for number in range(5))
    beta0 = jnp.sqrt(a / entries + EPSILON)
    alpha0 = (a + b) / (entries * beta0 * beta0)
    rest = 1.0 - alpha0
    square = (rest * rest * a + 2.0 * rest * b + d) / (beta0 * beta0)
    beta1 = jnp.sqrt(square / entries + EPSILON)
    mixed = (rest * rest * b + rest * (d + e) + f) / (beta0 * beta0)
    alpha1 = (square + mixed) / (entries * beta1 * beta1)
    back = ((rest * a + b) + (rest * b + e)) / (entries * beta0 * beta0 * beta1)
    scale = 1.0 / (beta0 * beta1)
    q2 = scale
    q1 = (1.0 + rest - alpha1) * scale
    q0 = (rest - alpha1 * rest) * scale - back / beta0
    top = lax.broadcasted_iota(jnp.int32, (8, 128), 0) == 0
    left = lax.broadcasted_iota(jnp.int32, (8, 128), 1) == 0
    table = jnp.where(top, jnp.where(left, alpha0, alpha1), jnp.where(left, beta0, beta1))
    coef_out[...] = table[0:2, 0:2]

    def finish(step, carry):
        at = pl.ds(pl.multiple_of(step * 512, 512), 512)

        def wide(q):
            return jnp.concatenate([q] * 4, axis=1)[None]

        vec_out[:, :, at] = (
            wide(q0) * uvec[0, :, :, at] + wide(q1) * uvec[1, :, :, at] + wide(q2) * uvec[2, :, :, at]
        ).astype(BF16)
        return carry

    lax.fori_loop(0, M * LEV // 512, finish, 0)

    for dlat, dlon in DIRECTIONS:

        def drain(dlat=dlat, dlon=dlon):
            input_copies(0, dlat, dlon).wait_send()
            input_copies(1, dlat, dlon).wait_send()
            z_copy(0, dlat, dlon).wait_send()
            z_copy(1, dlat, dlon).wait_send()
            if dlon == 0:
                param_copy(dlat).wait_send()

        inside(dlat, drain)
    for me, count, device, slots, send_sems, recv_sems in stages:
        for step in range(1, count):
            target = lax.rem(me + step, count)
            pltpu.make_async_remote_copy(
                src_ref=slots.at[me],
                dst_ref=slots.at[me],
                send_sem=send_sems.at[target],
                recv_sem=recv_sems.at[me],
                device_id=device(target),
                device_id_type=MESH,
            ).wait_send()


def per_device(topo, ensemble, innovation, obs_weight, lat_offset, lat_weight, band_widths):
    zh_n, x_n, zl_n, y_n, core_n = topo
    entries = float(4 * 8 * M * LEV * zh_n * x_n * zl_n * y_n * core_n)
    vmem = pltpu.VMEM
    dma = pltpu.SemaphoreType.DMA
    group_a, group_b, group_c = x_n * core_n, y_n, zh_n * zl_n
    anywhere = pl.BlockSpec(memory_space=pl.ANY)
    in_vmem = pl.BlockSpec(memory_space=pltpu.VMEM)
    return pl.pallas_call(
        functools.partial(kernel, topo, entries),
        out_shape=(
            jax.ShapeDtypeStruct((2, 2), F32),
            jax.ShapeDtypeStruct((4, 8, M * LEV), BF16),
        ),
        in_specs=[
            anywhere,
            anywhere,
            anywhere,
            in_vmem,
            in_vmem,
            pl.BlockSpec(memory_space=pltpu.SMEM),
        ],
        out_specs=(in_vmem, in_vmem),
        scratch_shapes=[
            vmem((4, 8, 2 * M * LEV), BF16),
            vmem((14, 40, 128), F32),
            vmem((14, 40, 128), F32),
            vmem((2, 2, 7, 16, 128), F32),
            vmem((2, 10, 24, 128), F32),
            vmem((3, 4, 8, 128), F32),
            vmem((3, 8, 128), F32),
            vmem((2, 5, 16, 128), F32),
            vmem((2, 4, 16, 128), F32),
            vmem((PAIRS, 128, 128), BF16),
            vmem((PAIRS, 128, 128), BF16),
            vmem((PAIRS, 128, 128), BF16),
            vmem((PAIRS, 8, 128), F32),
            vmem((3, 4, 8, M * LEV), F32),
            vmem((group_a, 1, 128), F32),
            vmem((group_b, 1, 128), F32),
            vmem((group_c, 1, 128), F32),
            dma((3,)),
            dma((2, 8)),
            dma((2, 8)),
            dma((2,)),
            dma((2,)),
            dma((2, 8)),
            dma((2, 8)),
            dma((group_a,)),
            dma((group_a,)),
            dma((group_b,)),
            dma((group_b,)),
            dma((group_c,)),
            dma((group_c,)),
        ],
        compiler_params=pltpu.CompilerParams(
            collective_id=0, has_side_effects=True, vmem_limit_bytes=32 * 1024 * 1024
        ),
        name="lanczos",
    )(
        ensemble,
        innovation,
        obs_weight,
        lat_offset.reshape(1, 16),
        lat_weight.reshape(1, 16),
        band_widths,
    )


def solution(mesh):
    return jax.shard_map(
        functools.partial(per_device, TOPO),
        mesh=mesh,
        in_specs=(
            P("lon", "lat", None),
            P("lon", "lat", None),
            P("lon", "lat", None),
            P("lat"),
            P("lat"),
            P(),
        ),
        out_specs=(P(), P("lon", "lat", None)),
        check_vma=False,
    )
```

profile of v0, /device:TPU:2, one launch (start us, length us, event | category | flops | bytes accessed | tf_op | source)
XLA Modules:
  0.0 72.3 jit_solution(13576225233071010282)
XLA Ops:
  0.6 0.0 copy-start.3
  0.6 0.0 copy-start.4
  0.7 0.0 copy-start.5
  0.7 0.6 copy-done.3
  1.3 0.0 copy-done.4
  1.3 0.0 copy-done.5
  1.3 0.0 copy-start
  1.3 1.1 %copy-done = bf16[4,8,10240]{2,1,0:T(8,128)(2,1)S(1)} copy-done((bf16[4,8,10240]{2,1,0:T(8,128)(2,1)S(1)}, bf16[4,8,10240]{2,1,0:T(8,128)(2,1)}, u32[]{:S(2)}) %copy-start) | copy-done | bytes 655384
  2.4 0.0 copy-start.1
  2.4 0.8 %copy-done.1 = f32[8,16,128]{2,1,0:T(8,128)S(1)} copy-done((f32[8,16,128]{2,1,0:T(8,128)S(1)}, f32[8,16,128]{2,1,0:T(8,128)}, u32[]{:S(2)}) %copy-start.1) | copy-done | bytes 65560
  3.2 0.0 copy-start.2
  3.2 0.8 %copy-done.2 = f32[8,16,128]{2,1,0:T(8,128)S(1)} copy-done((f32[8,16,128]{2,1,0:T(8,128)S(1)}, f32[8,16,128]{2,1,0:T(8,128)}, u32[]{:S(2)}) %copy-start.2) | copy-done | bytes 65560
  4.1 66.9 %lanczos.1 = (f32[2,2]{1,0:T(2,128)S(1)}, bf16[4,8,5120]{2,1,0:T(8,128)(2,1)S(1)}) custom-call(bf16[4,8,10240]{2,1,0:T(8,128)(2,1)S(1)} %copy-done, f32[8,16,128]{2,1,0:T(8,128)S(1)} %copy-done.1, f32[8,16,128]{2,1,0:T(8,128)S(1)} %copy-done.2, s32[1,16]{1,0:T(1,128)S(1)} %bitcast.2, f32[1,16]{1,0:T(1,128)S(1)} %bitcast.3, s32[80]{0:T(128)S(1)} %copy-done.5), custom_call_target="tpu_custom_call" | custom-call | tf_op jit(solution)/shard_map/lanczos/pallas_call | solution.py:452
  71.0 0.6 copy.10
  71.6 0.7 %copy.11 = bf16[4,8,5120]{2,1,0:T(8,128)(2,1)} copy(bf16[4,8,5120]{2,1,0:T(8,128)(2,1)S(1)} %get-tuple-element.5) | data formatting | bytes 655360
Async XLA Ops:
  0.6 0.7 copy-start.3
  0.6 0.7 copy-start.4
  0.7 0.7 copy-start.5
  1.3 1.1 %copy-start = (bf16[4,8,10240]{2,1,0:T(8,128)(2,1)S(1)}, bf16[4,8,10240]{2,1,0:T(8,128)(2,1)}, u32[]{:S(2)}) copy-start(bf16[4,8,10240]{2,1,0:T(8,128)(2,1)} %ens_hbm.1) | copy-start | bytes 1966084
  2.4 0.8 %copy-start.1 = (f32[8,16,128]{2,1,0:T(8,128)S(1)}, f32[8,16,128]{2,1,0:T(8,128)}, u32[]{:S(2)}) copy-start(f32[8,16,128]{2,1,0:T(8,128)} %innov_hbm.1) | copy-start | bytes 196612
  3.2 0.8 %copy-start.2 = (f32[8,16,128]{2,1,0:T(8,128)S(1)}, f32[8,16,128]{2,1,0:T(8,128)}, u32[]{:S(2)}) copy-start(f32[8,16,128]{2,1,0:T(8,128)} %wobs_hbm.1) | copy-start | bytes 196612
where the time goes:
time: 72.6 us; the launch traced here: 72.3 us
  Pallas kernels  66.9 us (92%)
  local copies, waits for them, and re-layouts  4.72 us (7%)
    pallas_call x1, Pallas kernels, per_device(): pl.pallas_call(functools.partial(kernel, topo, entries), out_shape=(jax.S...  66.9 us
    unnamed x14, local copies, waits for them, and re-layouts  4.72 us

commit v1 on v0

--- a/solution.py
+++ b/solution.py
@@ -18,7 +18,7 @@
 MESH = pl.DeviceIdType.MESH
 TOPO = (4, 4, 3, 8, 2)
 DIRECTIONS = ((1, 1), (1, -1), (-1, 1), (-1, -1), (1, 0), (-1, 0), (0, 1), (0, -1))
-UNROLL = 4
+UNROLL = 8
 
 
 def kernel(
@@ -27,13 +27,17 @@
     ens_hbm,
     innov_hbm,
     wobs_hbm,
+    offset_hbm,
+    weight_hbm,
+    bands_hbm,
+    table_out,
+    u_hbm,
     offset_ref,
     weight_ref,
     bands_ref,
-    coef_out,
-    vec_out,
     ens,
-    dext,
+    down,
+    fext,
     wext,
     wsplit,
     zext,
@@ -94,13 +98,22 @@
         (z_hi * zl_n + z_lo, zh_n * zl_n, dev_c, red_c, c_send, c_recv),
     )
 
-    dext[...] = jnp.zeros(dext.shape, F32)
+    small = [
+        pltpu.make_async_copy(src, dst, local_sem.at[3 + number])
+        for number, (src, dst) in enumerate(
+            ((bands_hbm, bands_ref), (weight_hbm, weight_ref), (offset_hbm, offset_ref))
+        )
+    ]
+    for copy in small:
+        copy.start()
+    own_d = pltpu.make_async_copy(innov_hbm, down, local_sem.at[0])
+    own_w = pltpu.make_async_copy(wobs_hbm, wext.at[3:11, 8:24], local_sem.at[1])
+    own_e = pltpu.make_async_copy(ens_hbm, ens, local_sem.at[2])
+
+    fext[...] = jnp.zeros(fext.shape, F32)
     wext[...] = jnp.zeros(wext.shape, F32)
     zext[...] = jnp.zeros(zext.shape, F32)
     params[...] = jnp.zeros(params.shape, F32)
-    params[1, 0:1, 0:16] = weight_ref[...]
-    params[1, 1:2, 0:16] = offset_ref[...].astype(F32)
-
     barrier = pltpu.get_barrier_semaphore()
     for dlat, dlon in DIRECTIONS:
 
@@ -119,12 +132,13 @@
                 device_id_type=MESH,
             )
 
-    own_d = pltpu.make_async_copy(innov_hbm, dext.at[3:11, 8:24], local_sem.at[0])
-    own_w = pltpu.make_async_copy(wobs_hbm, wext.at[3:11, 8:24], local_sem.at[1])
-    own_e = pltpu.make_async_copy(ens_hbm, ens, local_sem.at[2])
     own_d.start()
     own_w.start()
     own_e.start()
+    for copy in small:
+        copy.wait()
+    params[1, 0:1, 0:16] = weight_ref[...]
+    params[1, 1:2, 0:16] = offset_ref[...].astype(F32)
 
     rows = lax.broadcasted_iota(jnp.int32, (128, 128), 0)
     cols = lax.broadcasted_iota(jnp.int32, (128, 128), 1)
@@ -132,8 +146,8 @@
     distance = jnp.where(same, jnp.abs(rows - cols), 1000)
     first_half = lax.broadcasted_iota(jnp.int32, (1, 128), 1) < LEV
 
-    def build(j, carry):
-        width = jnp.where(first_half, bands_ref[2 * j] + 1, bands_ref[2 * j + 1] + 1)
+    def build(j):
+        width = jnp.where(first_half, bands_ref[0, 2 * j] + 1, bands_ref[0, 2 * j + 1] + 1)
         tent = jnp.maximum(width - distance, 0).astype(F32).astype(BF16)
         wide = width.astype(F32)
         scale = 1.0 / (wide * wide)
@@ -143,10 +157,17 @@
         sq_hi[j] = high
         sq_lo[j] = (square - high.astype(F32)).astype(BF16)
         inv2[j] = jnp.broadcast_to(scale, (8, 128))
+
+    def build_some(step, carry):
+        for extra in range(UNROLL):
+            build(step * UNROLL + extra)
         return carry
 
-    lax.fori_loop(0, PAIRS, build, 0)
-
+    lax.fori_loop(0, PAIRS // UNROLL, build_some, 0)
+
+    own_d.wait()
+    own_w.wait()
+    fext[3:11, 8:24, :] = down[...] * wext[3:11, 8:24, :]
     edges = (lat == 0).astype(jnp.int32) + (lat == lat_n - 1).astype(jnp.int32)
     others = sum(count - 1 for _, count, _, _, _, _ in stages)
     pl.semaphore_wait(barrier, others + 8 - 3 * edges)
@@ -158,14 +179,19 @@
             return slice(size - width, size), slice(before - width, before)
         return slice(0, width), slice(before + size, before + size + width)
 
-    def input_copies(which, dlat, dlon):
+    def shifted(part, by):
+        return slice(part.start + by, part.stop + by)
+
+    def input_copy(which, dlat, dlon):
         src_cols, dst_cols = cut(dlon, 8, 3, 3)
-        src_rows, dst_rows = cut(dlat, 16, 8, 8)
+        src_rows, dst_rows = cut(dlat, 16, 4, 8)
         number = DIRECTIONS.index((dlat, dlon))
-        pairs = ((innov_hbm, dext), (wobs_hbm, wext))
-        src, dst = pairs[which]
+        if which == 0:
+            src, dst = fext.at[shifted(src_cols, 3), shifted(src_rows, 8)], fext
+        else:
+            src, dst = wobs_hbm.at[src_cols, src_rows], wext
         return pltpu.make_async_remote_copy(
-            src_ref=src.at[src_cols, src_rows],
+            src_ref=src,
             dst_ref=dst.at[dst_cols, dst_rows],
             send_sem=in_send.at[which, number],
             recv_sem=in_recv.at[which, number],
@@ -185,12 +211,10 @@
 
     def z_copy(phase, dlat, dlon):
         src_cols, dst_cols = cut(dlon, 4, 3, 3)
-        src_rows, dst_rows = cut(dlat, 8, 8, 8)
+        src_rows, dst_rows = cut(dlat, 8, 4, 8)
         number = DIRECTIONS.index((dlat, dlon))
-        src_cols = slice(src_cols.start + 3, src_cols.stop + 3)
-        src_rows = slice(src_rows.start + 8, src_rows.stop + 8)
         return pltpu.make_async_remote_copy(
-            src_ref=zext.at[phase, src_cols, src_rows],
+            src_ref=zext.at[phase, shifted(src_cols, 3), shifted(src_rows, 8)],
             dst_ref=zext.at[phase, dst_cols, dst_rows],
             send_sem=z_send.at[phase, number],
             recv_sem=z_recv.at[phase, number],
@@ -198,28 +222,24 @@
             device_id_type=MESH,
         )
 
-    for dlat, dlon in DIRECTIONS:
-
-        def send(dlat=dlat, dlon=dlon):
-            input_copies(0, dlat, dlon).start()
-            input_copies(1, dlat, dlon).start()
-            if dlon == 0:
-                param_copy(dlat).start()
-
-        inside(dlat, send)
-
-    own_d.wait()
-    own_w.wait()
-    own_e.wait()
-    for dlat, dlon in DIRECTIONS:
-
-        def receive(dlat=dlat, dlon=dlon):
-            input_copies(0, dlat, dlon).wait_recv()
-            input_copies(1, dlat, dlon).wait_recv()
-            if dlon == 0:
-                param_copy(dlat).wait_recv()
-
-        inside(-dlat, receive)
+    for dlat in (-1, 1):
+        inside(dlat, lambda dlat=dlat: param_copy(dlat).start())
+    for which in range(2):
+        for dlat, dlon in DIRECTIONS:
+            inside(
+                dlat,
+                lambda which=which, dlat=dlat, dlon=dlon: input_copy(which, dlat, dlon).start(),
+            )
+
+    def receive_input(which):
+        for dlat, dlon in DIRECTIONS:
+            inside(
+                -dlat,
+                lambda dlat=dlat, dlon=dlon: input_copy(which, dlat, dlon).wait_recv(),
+            )
+
+    for dlat in (-1, 1):
+        inside(-dlat, lambda dlat=dlat: param_copy(dlat).wait_recv())
 
     row = lax.broadcasted_iota(jnp.int32, (16, 128), 0)
     lane = lax.broadcasted_iota(jnp.int32, (16, 128), 1)
@@ -255,17 +275,12 @@
                 )
         return result
 
+    def split_rows(ext, parity, kind):
+        at = pl.ds(4 + parity, 16, stride=2)
+        return jnp.stack([ext[2 * b + kind, at, :] for b in range(7)])
+
     def start_field(parity):
-        found = []
-        for kind in range(2):
-            column = []
-            for b in range(7):
-                at = pl.ds(4 + parity, 16, stride=2)
-                weight = wext[2 * b + kind, at, :]
-                wsplit[parity, kind, b] = weight
-                column.append(weight * dext[2 * b + kind, at, :])
-            found.append(jnp.stack(column))
-        return found
+        return [split_rows(fext, parity, kind) for kind in range(2)]
 
     def fine_field(phase):
         def field(parity):
@@ -285,7 +300,7 @@
     first_lanes = lax.broadcasted_iota(jnp.int32, (4, 8, 128), 2) < LEV
 
     def split_pair(j, y):
-        at = pl.multiple_of(j * 256, 256)
+        at = j * 256 if isinstance(j, int) else pl.multiple_of(j * 256, 256)
         e0 = ens[:, :, pl.ds(at, 128)].astype(F32)
         e1 = ens[:, :, pl.ds(at + 128, 128)].astype(F32)
         p0, p1 = e0 * y, e1 * y
@@ -297,20 +312,17 @@
         return e0, e1, high, low
 
     def combine_spread(y):
-        def body(step, acc):
-            for extra in range(UNROLL):
-                j = step * UNROLL + extra
-                e0, e1, high, low = split_pair(j, y)
-                both = jnp.concatenate([high, low], axis=0)
-                main = jnp.dot(both, sq_hi[j], preferred_element_type=F32)
-                rest = jnp.dot(high, sq_lo[j], preferred_element_type=F32)
-                out = (main[:32] + (main[32:] + rest)).reshape(4, 8, 128)
-                turned = pltpu.roll(out, LEV, 2)
-                acc = acc + e0 * jnp.where(first_lanes, out, turned)
-                acc = acc + e1 * jnp.where(first_lanes, turned, out)
-            return acc
-
-        return lax.fori_loop(0, PAIRS // UNROLL, body, jnp.zeros((4, 8, 128), F32))
+        acc = jnp.zeros((4, 8, 128), F32)
+        for j in range(PAIRS):
+            e0, e1, high, low = split_pair(j, y)
+            both = jnp.concatenate([high, low], axis=0)
+            main = jnp.dot(both, sq_hi[j], preferred_element_type=F32)
+            rest = jnp.dot(high, sq_lo[j], preferred_element_type=F32)
+            out = (main[:32] + (main[32:] + rest)).reshape(4, 8, 128)
+            turned = pltpu.roll(out, LEV, 2)
+            acc = acc + e0 * jnp.where(first_lanes, out, turned)
+            acc = acc + e1 * jnp.where(first_lanes, turned, out)
+        return acc
 
     def spread(which):
         y = yv[which]
@@ -327,6 +339,8 @@
 
         lax.fori_loop(0, PAIRS // UNROLL, body, 0)
 
+    own_e.wait()
+    receive_input(0)
     yv[0] = restrict(start_field)
 
     for phase in range(2):
@@ -339,6 +353,12 @@
 
             inside(dlat, send)
         spread(phase)
+        pltpu.make_async_copy(uvec.at[phase], u_hbm.at[phase], local_sem.at[6 + phase]).start()
+        if phase == 0:
+            receive_input(1)
+            for parity in range(2):
+                for kind in range(2):
+                    wsplit[parity, kind] = split_rows(wext, parity, kind)
         for dlat, dlon in DIRECTIONS:
 
             def receive(dlat=dlat, dlon=dlon, phase=phase):
@@ -347,14 +367,10 @@
             inside(-dlat, receive)
         yv[phase + 1] = restrict(fine_field(phase))
 
-    z0, z1 = zext[0, 3:7, 8:16, :], zext[1, 3:7, 8:16, :]
-    y0, y1, y2 = yv[0], yv[1], yv[2]
     lane1 = lax.broadcasted_iota(jnp.int32, (1, 128), 1)
     local = jnp.zeros((1, 128), F32)
-    for number, (left, right) in enumerate(
-        ((z0, y0), (z0, y1), (z1, y1), (z0, y2), (z1, y2))
-    ):
-        plane = jnp.sum(left * right, axis=0)
+    for number, (left, right) in enumerate(((0, 0), (0, 1), (1, 1), (0, 2), (1, 2))):
+        plane = jnp.sum(zext[left, 3:7, 8:16, :] * yv[right], axis=0)
         value = jnp.sum(jnp.sum(plane, axis=0, keepdims=True), axis=1, keepdims=True)
         local = local + jnp.where(lane1 == number, jnp.broadcast_to(value, (1, 128)), 0.0)
 
@@ -375,6 +391,7 @@
             stage_copy(lax.rem(me + step, count), me).start()
         if number == 0:
             spread(2)
+            pltpu.make_async_copy(uvec.at[2], u_hbm.at[2], local_sem.at[8]).start()
         for step in range(1, count):
             other = lax.rem(me + step, count)
             stage_copy(other, other).wait_recv()
@@ -399,33 +416,23 @@
     q2 = scale
     q1 = (1.0 + rest - alpha1) * scale
     q0 = (rest - alpha1 * rest) * scale - back / beta0
-    top = lax.broadcasted_iota(jnp.int32, (8, 128), 0) == 0
+    row8 = lax.broadcasted_iota(jnp.int32, (8, 128), 0)
     left = lax.broadcasted_iota(jnp.int32, (8, 128), 1) == 0
-    table = jnp.where(top, jnp.where(left, alpha0, alpha1), jnp.where(left, beta0, beta1))
-    coef_out[...] = table[0:2, 0:2]
-
-    def finish(step, carry):
-        at = pl.ds(pl.multiple_of(step * 512, 512), 512)
-
-        def wide(q):
-            return jnp.concatenate([q] * 4, axis=1)[None]
-
-        vec_out[:, :, at] = (
-            wide(q0) * uvec[0, :, :, at] + wide(q1) * uvec[1, :, :, at] + wide(q2) * uvec[2, :, :, at]
-        ).astype(BF16)
-        return carry
-
-    lax.fori_loop(0, M * LEV // 512, finish, 0)
-
+    table = jnp.where(row8 == 0, jnp.where(left, alpha0, alpha1), jnp.where(left, beta0, beta1))
+    for number, q in enumerate((q0, q1, q2)):
+        table = jnp.where(row8 == 2 + number, q, table)
+    table_out[...] = table
+
+    for number in range(3):
+        pltpu.make_async_copy(uvec.at[number], u_hbm.at[number], local_sem.at[6 + number]).wait()
+    for dlat in (-1, 1):
+        inside(dlat, lambda dlat=dlat: param_copy(dlat).wait_send())
     for dlat, dlon in DIRECTIONS:
 
         def drain(dlat=dlat, dlon=dlon):
-            input_copies(0, dlat, dlon).wait_send()
-            input_copies(1, dlat, dlon).wait_send()
-            z_copy(0, dlat, dlon).wait_send()
-            z_copy(1, dlat, dlon).wait_send()
-            if dlon == 0:
-                param_copy(dlat).wait_send()
+            for which in range(2):
+                input_copy(which, dlat, dlon).wait_send()
+                z_copy(which, dlat, dlon).wait_send()
 
         inside(dlat, drain)
     for me, count, device, slots, send_sems, recv_sems in stages:
@@ -441,6 +448,32 @@
             ).wait_send()
 
 
+def finish(table_hbm, u_hbm, coef_hbm, vec_hbm, table, corner, u, vec, sems):
+    head = pltpu.make_async_copy(table_hbm, table, sems.at[0, 4])
+    tail = pltpu.make_async_copy(corner, coef_hbm, sems.at[1, 4])
+    loads = [pltpu.make_async_copy(u_hbm.at[:, c], u.at[:, c], sems.at[0, c]) for c in range(4)]
+    stores = [pltpu.make_async_copy(vec.at[c], vec_hbm.at[c], sems.at[1, c]) for c in range(4)]
+    head.start()
+    for load in loads:
+        load.start()
+    head.wait()
+    corner[...] = table[0:2, 0:2]
+    tail.start()
+    q = [jnp.broadcast_to(table[2 + k : 3 + k, :], (8, 128)) for k in range(3)]
+    wide = [jnp.concatenate([part] * 8, axis=1) for part in q]
+    for c in range(4):
+        loads[c].wait()
+        for step in range(M * LEV // 1024):
+            at = slice(step * 1024, (step + 1) * 1024)
+            vec[c, :, at] = (
+                wide[0] * u[0, c, :, at] + wide[1] * u[1, c, :, at] + wide[2] * u[2, c, :, at]
+            ).astype(BF16)
+        stores[c].start()
+    for store in stores:
+        store.wait()
+    tail.wait()
+
+
 def per_device(topo, ensemble, innovation, obs_weight, lat_offset, lat_weight, band_widths):
     zh_n, x_n, zl_n, y_n, core_n = topo
     entries = float(4 * 8 * M * LEV * zh_n * x_n * zl_n * y_n * core_n)
@@ -449,23 +482,27 @@
     group_a, group_b, group_c = x_n * core_n, y_n, zh_n * zl_n
     anywhere = pl.BlockSpec(memory_space=pl.ANY)
     in_vmem = pl.BlockSpec(memory_space=pltpu.VMEM)
-    return pl.pallas_call(
+    table, u = pl.pallas_call(
         functools.partial(kernel, topo, entries),
         out_shape=(
-            jax.ShapeDtypeStruct((2, 2), F32),
-            jax.ShapeDtypeStruct((4, 8, M * LEV), BF16),
+            jax.ShapeDtypeStruct((8, 128), F32),
+            jax.ShapeDtypeStruct((3, 4, 8, M * LEV), F32),
         ),
         in_specs=[
             anywhere,
             anywhere,
             anywhere,
-            in_vmem,
-            in_vmem,
-            pl.BlockSpec(memory_space=pltpu.SMEM),
+            anywhere,
+            anywhere,
+            anywhere,
         ],
-        out_specs=(in_vmem, in_vmem),
+        out_specs=(in_vmem, anywhere),
         scratch_shapes=[
+            vmem((1, 16), jnp.int32),
+            vmem((1, 16), F32),
+            pltpu.SMEM((1, M), jnp.int32),
             vmem((4, 8, 2 * M * LEV), BF16),
+            vmem((8, 16, 128), F32),
             vmem((14, 40, 128), F32),
             vmem((14, 40, 128), F32),
             vmem((2, 2, 7, 16, 128), F32),
@@ -482,7 +519,7 @@
             vmem((group_a, 1, 128), F32),
             vmem((group_b, 1, 128), F32),
             vmem((group_c, 1, 128), F32),
-            dma((3,)),
+            dma((9,)),
             dma((2, 8)),
             dma((2, 8)),
             dma((2,)),
@@ -497,7 +534,7 @@
             dma((group_c,)),
         ],
         compiler_params=pltpu.CompilerParams(
-            collective_id=0, has_side_effects=True, vmem_limit_bytes=32 * 1024 * 1024
+            collective_id=0, has_side_effects=True, vmem_limit_bytes=62 * 1024 * 1024
         ),
         name="lanczos",
     )(
@@ -506,8 +543,26 @@
         obs_weight,
         lat_offset.reshape(1, 16),
         lat_weight.reshape(1, 16),
-        band_widths,
+        band_widths.reshape(1, M),
     )
+    return pl.pallas_call(
+        finish,
+        out_shape=(
+            jax.ShapeDtypeStruct((2, 2), F32),
+            jax.ShapeDtypeStruct((4, 8, M * LEV), BF16),
+        ),
+        in_specs=[anywhere, anywhere],
+        out_specs=(anywhere, anywhere),
+        scratch_shapes=[
+            vmem((8, 128), F32),
+            vmem((2, 2), F32),
+            vmem((3, 4, 8, M * LEV), F32),
+            vmem((4, 8, M * LEV), BF16),
+            dma((2, 5)),
+        ],
+        compiler_params=pltpu.CompilerParams(vmem_limit_bytes=62 * 1024 * 1024),
+        name="finish",
+    )(table, u)
 
 
 def solution(mesh):

time: 72.6 us -> 58.8 us (0.81)
  Pallas kernels: 66.9 us -> 57.9 us
  local copies, waits for them, and re-layouts: 4.72 us -> 0 us
    pallas_call x1, Pallas kernels: 66.9 us -> 55.7 us  [per_device(): pl.pallas_call(functools.partial(kernel, topo, entries), out_shape=(jax.S...]
    unnamed x14 -> x0, local copies, waits for them, and re-layouts: 4.72 us -> none
    pallas_call x0 -> x1, Pallas kernels: none -> 2.23 us  [per_device(): pl.pallas_call(finish, out_shape=(jax.ShapeDtypeStruct((2, 2), F32), jax....]
where the time goes in v1:
time: 58.8 us; the launch traced here: 58.6 us
  Pallas kernels  57.9 us (98%)
  between operations  0.64 us (1%)
    pallas_call x1, Pallas kernels, per_device(): pl.pallas_call(functools.partial(kernel, topo, entries), out_shape=(jax.S...  55.7 us
    pallas_call x1, Pallas kernels, per_device(): pl.pallas_call(finish, out_shape=(jax.ShapeDtypeStruct((2, 2), F32), jax....  2.23 us

profile of v1, /device:TPU:2, one launch (start us, length us, event | category | flops | bytes accessed | tf_op | source)
XLA Modules:
  0.0 58.6 jit_solution(5777104450063580336)
XLA Ops:
  0.6 55.7 %lanczos.1 = (f32[8,128]{1,0:T(8,128)}, f32[3,4,8,5120]{3,2,1,0:T(8,128)}) custom-call(bf16[4,8,10240]{2,1,0:T(8,128)(2,1)} %ens_hbm.1, f32[8,16,128]{2,1,0:T(8,128)} %innov_hbm.1, f32[8,16,128]{2,1,0:T(8,128)} %wobs_hbm.1, s32[1,16]{1,0:T(1,128)} %bitcast.3, f32[1,16]{1,0:T(1,128)} %bitcast.4, s32[1,80]{1,0:T(1,128)} %bitcast.5), custom_call_target="tpu_custom_call" | custom-call | tf_op jit(solution)/shard_map/lanczos/pallas_call | solution.py:485
  56.3 2.2 %finish.1 = (f32[2,2]{1,0:T(2,128)}, bf16[4,8,5120]{2,1,0:T(8,128)(2,1)}) custom-call(f32[8,128]{1,0:T(8,128)} %get-tuple-element.4.table_hbm, f32[3,4,8,5120]{3,2,1,0:T(8,128)} %get-tuple-element.5.u_hbm), custom_call_target="tpu_custom_call" | custom-call | tf_op jit(solution)/shard_map/finish/pallas_call | solution.py:548

commit v2 on v1

--- a/solution.py
+++ b/solution.py
@@ -31,13 +31,16 @@
     weight_hbm,
     bands_hbm,
     table_out,
-    u_hbm,
+    uvec,
     offset_ref,
     weight_ref,
     bands_ref,
     ens,
     down,
-    fext,
+    fown,
+    hbuf,
+    ybuf,
+    yin,
     wext,
     wsplit,
     zext,
@@ -49,7 +52,6 @@
     sq_hi,
     sq_lo,
     inv2,
-    uvec,
     red_a,
     red_b,
     red_c,
@@ -110,7 +112,9 @@
     own_w = pltpu.make_async_copy(wobs_hbm, wext.at[3:11, 8:24], local_sem.at[1])
     own_e = pltpu.make_async_copy(ens_hbm, ens, local_sem.at[2])
 
-    fext[...] = jnp.zeros(fext.shape, F32)
+    fown[...] = jnp.zeros(fown.shape, F32)
+    hbuf[...] = jnp.zeros(hbuf.shape, F32)
+    yin[...] = jnp.zeros(yin.shape, F32)
     wext[...] = jnp.zeros(wext.shape, F32)
     zext[...] = jnp.zeros(zext.shape, F32)
     params[...] = jnp.zeros(params.shape, F32)
@@ -167,7 +171,48 @@
 
     own_d.wait()
     own_w.wait()
-    fext[3:11, 8:24, :] = down[...] * wext[3:11, 8:24, :]
+    fown[:, 8:24, :] = down[...] * wext[3:11, 8:24, :]
+
+    row = lax.broadcasted_iota(jnp.int32, (16, 128), 0)
+    lane = lax.broadcasted_iota(jnp.int32, (16, 128), 1)
+
+    def find_coef(sources):
+        for parity in range(2):
+            fine = 2 * row - 4 + parity
+            picked = []
+            for kind in range(2):
+                total = jnp.zeros((16, 128), F32)
+                for source in sources:
+                    line = jnp.broadcast_to(params[source, kind : kind + 1, :], (16, 128))
+                    total = total + jnp.where(lane == fine + 16 - 16 * source, line, 0.0)
+                picked.append(
+                    jnp.broadcast_to(jnp.sum(total, axis=1, keepdims=True), (16, 128))
+                )
+            upper, offset = picked
+            for k in range(5):
+                coef[parity, k] = jnp.where(offset == float(k), 1.0 - upper, 0.0) + jnp.where(
+                    offset == float(k - 1), upper, 0.0
+                )
+
+    find_coef((1,))
+    shares = [jnp.zeros((8, 16, 128), F32) for _ in range(5)]
+    for parity in range(2):
+        at = pl.ds(4 + parity, 16, stride=2)
+        columns = [jnp.zeros((16, 128), F32) for _ in range(8)]
+        for c in range(4):
+            even, odd = fown[2 * c, at, :], fown[2 * c + 1, at, :]
+            for t in range(4):
+                columns[c + t] = columns[c + t] + EVEN_TAPS[t] * even
+                columns[c + 1 + t] = columns[c + 1 + t] + ODD_TAPS[t] * odd
+        along = jnp.stack(columns)
+        shares = [shares[k] + coef[parity, k][None] * along for k in range(5)]
+    for k in range(5):
+        hbuf[k, :, 8:24, :] = shares[k]
+    total = jnp.zeros((8, 24, 128), F32)
+    for k in range(5):
+        total = total + hbuf[k, :, 4 - k : 28 - k, :]
+    ybuf[...] = total
+
     edges = (lat == 0).astype(jnp.int32) + (lat == lat_n - 1).astype(jnp.int32)
     others = sum(count - 1 for _, count, _, _, _, _ in stages)
     pl.semaphore_wait(barrier, others + 8 - 3 * edges)
@@ -182,19 +227,36 @@
     def shifted(part, by):
         return slice(part.start + by, part.stop + by)
 
-    def input_copy(which, dlat, dlon):
+    def weight_copy(dlat, dlon):
         src_cols, dst_cols = cut(dlon, 8, 3, 3)
         src_rows, dst_rows = cut(dlat, 16, 4, 8)
         number = DIRECTIONS.index((dlat, dlon))
-        if which == 0:
-            src, dst = fext.at[shifted(src_cols, 3), shifted(src_rows, 8)], fext
-        else:
-            src, dst = wobs_hbm.at[src_cols, src_rows], wext
         return pltpu.make_async_remote_copy(
-            src_ref=src,
-            dst_ref=dst.at[dst_cols, dst_rows],
-            send_sem=in_send.at[which, number],
-            recv_sem=in_recv.at[which, number],
+            src_ref=wobs_hbm.at[src_cols, src_rows],
+            dst_ref=wext.at[dst_cols, dst_rows],
+            send_sem=in_send.at[1, number],
+            recv_sem=in_recv.at[1, number],
+            device_id=neighbour(dlat, dlon),
+            device_id_type=MESH,
+        )
+
+    def share_copy(dlat, dlon):
+        number = DIRECTIONS.index((dlat, dlon))
+        src_cols, dst_cols = (
+            (slice(2, 6), slice(0, 4)),
+            (slice(6, 8), slice(0, 2)),
+            (slice(0, 2), slice(2, 4)),
+        )[dlon]
+        src_rows, dst_rows = (
+            (slice(8, 16), slice(0, 8)),
+            (slice(16, 18), slice(0, 2)),
+            (slice(6, 8), slice(6, 8)),
+        )[dlat]
+        return pltpu.make_async_remote_copy(
+            src_ref=ybuf.at[src_cols, src_rows],
+            dst_ref=yin.at[number, dst_cols, dst_rows],
+            send_sem=in_send.at[0, number],
+            recv_sem=in_recv.at[0, number],
             device_id=neighbour(dlat, dlon),
             device_id_type=MESH,
         )
@@ -222,65 +284,31 @@
             device_id_type=MESH,
         )
 
+    for dlat, dlon in DIRECTIONS:
+        inside(dlat, lambda dlat=dlat, dlon=dlon: share_copy(dlat, dlon).start())
     for dlat in (-1, 1):
         inside(dlat, lambda dlat=dlat: param_copy(dlat).start())
-    for which in range(2):
-        for dlat, dlon in DIRECTIONS:
-            inside(
-                dlat,
-                lambda which=which, dlat=dlat, dlon=dlon: input_copy(which, dlat, dlon).start(),
-            )
-
-    def receive_input(which):
-        for dlat, dlon in DIRECTIONS:
-            inside(
-                -dlat,
-                lambda dlat=dlat, dlon=dlon: input_copy(which, dlat, dlon).wait_recv(),
-            )
-
-    for dlat in (-1, 1):
-        inside(-dlat, lambda dlat=dlat: param_copy(dlat).wait_recv())
-
-    row = lax.broadcasted_iota(jnp.int32, (16, 128), 0)
-    lane = lax.broadcasted_iota(jnp.int32, (16, 128), 1)
-    for parity in range(2):
-        fine = 2 * row - 4 + parity
-        picked = []
-        for kind in range(2):
-            total = jnp.zeros((16, 128), F32)
-            for source in range(3):
-                line = jnp.broadcast_to(params[source, kind : kind + 1, :], (16, 128))
-                total = total + jnp.where(lane == fine + 16 - 16 * source, line, 0.0)
-            picked.append(
-                jnp.broadcast_to(jnp.sum(total, axis=1, keepdims=True), (16, 128))
-            )
-        upper, offset = picked
-        for k in range(5):
-            coef[parity, k] = jnp.where(offset == float(k), 1.0 - upper, 0.0) + jnp.where(
-                offset == float(k - 1), upper, 0.0
-            )
+    for dlat, dlon in DIRECTIONS:
+        inside(dlat, lambda dlat=dlat, dlon=dlon: weight_copy(dlat, dlon).start())
 
     def restrict(fields):
+        shares = [jnp.zeros((4, 16, 128), F32) for _ in range(5)]
         for parity in range(2):
             odd, even = fields(parity)
             total = jnp.zeros((4, 16, 128), F32)
             for t in range(4):
                 total = total + ODD_TAPS[t] * odd[3 - t : 7 - t] + EVEN_TAPS[t] * even[3 - t : 7 - t]
-            gbuf[parity] = total
+            shares = [shares[k] + coef[parity, k][None] * total for k in range(5)]
+        for k in range(5):
+            gbuf[k] = shares[k]
         result = jnp.zeros((4, 8, 128), F32)
-        for parity in range(2):
-            for k in range(5):
-                result = result + (
-                    coef[parity, k, 4 - k : 12 - k, :][None] * gbuf[parity, :, 4 - k : 12 - k, :]
-                )
+        for k in range(5):
+            result = result + gbuf[k, :, 4 - k : 12 - k, :]
         return result
 
-    def split_rows(ext, parity, kind):
+    def split_rows(parity, kind):
         at = pl.ds(4 + parity, 16, stride=2)
-        return jnp.stack([ext[2 * b + kind, at, :] for b in range(7)])
-
-    def start_field(parity):
-        return [split_rows(fext, parity, kind) for kind in range(2)]
+        return jnp.stack([wext[2 * b + kind, at, :] for b in range(7)])
 
     def fine_field(phase):
         def field(parity):
@@ -340,8 +368,12 @@
         lax.fori_loop(0, PAIRS // UNROLL, body, 0)
 
     own_e.wait()
-    receive_input(0)
-    yv[0] = restrict(start_field)
+    for dlat, dlon in DIRECTIONS:
+        inside(-dlat, lambda dlat=dlat, dlon=dlon: share_copy(dlat, dlon).wait_recv())
+    start = ybuf[2:6, 8:16, :]
+    for number in range(8):
+        start = start + yin[number]
+    yv[0] = start
 
     for phase in range(2):
         z = combine_spread(yv[phase])
@@ -353,12 +385,15 @@
 
             inside(dlat, send)
         spread(phase)
-        pltpu.make_async_copy(uvec.at[phase], u_hbm.at[phase], local_sem.at[6 + phase]).start()
         if phase == 0:
-            receive_input(1)
+            for dlat in (-1, 1):
+                inside(-dlat, lambda dlat=dlat: param_copy(dlat).wait_recv())
+            find_coef((0, 1, 2))
+            for dlat, dlon in DIRECTIONS:
+                inside(-dlat, lambda dlat=dlat, dlon=dlon: weight_copy(dlat, dlon).wait_recv())
             for parity in range(2):
                 for kind in range(2):
-                    wsplit[parity, kind] = split_rows(wext, parity, kind)
+                    wsplit[parity, kind] = split_rows(parity, kind)
         for dlat, dlon in DIRECTIONS:
 
             def receive(dlat=dlat, dlon=dlon, phase=phase):
@@ -391,7 +426,6 @@
             stage_copy(lax.rem(me + step, count), me).start()
         if number == 0:
             spread(2)
-            pltpu.make_async_copy(uvec.at[2], u_hbm.at[2], local_sem.at[8]).start()
         for step in range(1, count):
             other = lax.rem(me + step, count)
             stage_copy(other, other).wait_recv()
@@ -423,16 +457,15 @@
         table = jnp.where(row8 == 2 + number, q, table)
     table_out[...] = table
 
-    for number in range(3):
-        pltpu.make_async_copy(uvec.at[number], u_hbm.at[number], local_sem.at[6 + number]).wait()
     for dlat in (-1, 1):
         inside(dlat, lambda dlat=dlat: param_copy(dlat).wait_send())
     for dlat, dlon in DIRECTIONS:
 
         def drain(dlat=dlat, dlon=dlon):
-            for which in range(2):
-                input_copy(which, dlat, dlon).wait_send()
-                z_copy(which, dlat, dlon).wait_send()
+            share_copy(dlat, dlon).wait_send()
+            weight_copy(dlat, dlon).wait_send()
+            z_copy(0, dlat, dlon).wait_send()
+            z_copy(1, dlat, dlon).wait_send()
 
         inside(dlat, drain)
     for me, count, device, slots, send_sems, recv_sems in stages:
@@ -448,21 +481,14 @@
             ).wait_send()
 
 
-def finish(table_hbm, u_hbm, coef_hbm, vec_hbm, table, corner, u, vec, sems):
-    head = pltpu.make_async_copy(table_hbm, table, sems.at[0, 4])
-    tail = pltpu.make_async_copy(corner, coef_hbm, sems.at[1, 4])
-    loads = [pltpu.make_async_copy(u_hbm.at[:, c], u.at[:, c], sems.at[0, c]) for c in range(4)]
-    stores = [pltpu.make_async_copy(vec.at[c], vec_hbm.at[c], sems.at[1, c]) for c in range(4)]
-    head.start()
-    for load in loads:
-        load.start()
-    head.wait()
+def finish(table, u, coef_hbm, vec_hbm, corner, vec, sems):
     corner[...] = table[0:2, 0:2]
+    tail = pltpu.make_async_copy(corner, coef_hbm, sems.at[4])
     tail.start()
+    stores = [pltpu.make_async_copy(vec.at[c], vec_hbm.at[c], sems.at[c]) for c in range(4)]
     q = [jnp.broadcast_to(table[2 + k : 3 + k, :], (8, 128)) for k in range(3)]
     wide = [jnp.concatenate([part] * 8, axis=1) for part in q]
     for c in range(4):
-        loads[c].wait()
         for step in range(M * LEV // 1024):
             at = slice(step * 1024, (step + 1) * 1024)
             vec[c, :, at] = (
@@ -496,30 +522,32 @@
             anywhere,
             anywhere,
         ],
-        out_specs=(in_vmem, anywhere),
+        out_specs=(in_vmem, in_vmem),
         scratch_shapes=[
             vmem((1, 16), jnp.int32),
             vmem((1, 16), F32),
             pltpu.SMEM((1, M), jnp.int32),
             vmem((4, 8, 2 * M * LEV), BF16),
             vmem((8, 16, 128), F32),
-            vmem((14, 40, 128), F32),
+            vmem((8, 40, 128), F32),
+            vmem((5, 8, 32, 128), F32),
+            vmem((8, 24, 128), F32),
+            vmem((8, 4, 8, 128), F32),
             vmem((14, 40, 128), F32),
             vmem((2, 2, 7, 16, 128), F32),
             vmem((2, 10, 24, 128), F32),
             vmem((3, 4, 8, 128), F32),
             vmem((3, 8, 128), F32),
             vmem((2, 5, 16, 128), F32),
-            vmem((2, 4, 16, 128), F32),
+            vmem((5, 4, 16, 128), F32),
             vmem((PAIRS, 128, 128), BF16),
             vmem((PAIRS, 128, 128), BF16),
             vmem((PAIRS, 128, 128), BF16),
             vmem((PAIRS, 8, 128), F32),
-            vmem((3, 4, 8, M * LEV), F32),
             vmem((group_a, 1, 128), F32),
             vmem((group_b, 1, 128), F32),
             vmem((group_c, 1, 128), F32),
-            dma((9,)),
+            dma((6,)),
             dma((2, 8)),
             dma((2, 8)),
             dma((2,)),
@@ -534,16 +562,21 @@
             dma((group_c,)),
         ],
         compiler_params=pltpu.CompilerParams(
-            collective_id=0, has_side_effects=True, vmem_limit_bytes=62 * 1024 * 1024
+            collective_id=0, has_side_effects=True, vmem_limit_bytes=24 * 1024 * 1024
         ),
         name="lanczos",
     )(
-        ensemble,
-        innovation,
-        obs_weight,
-        lat_offset.reshape(1, 16),
-        lat_weight.reshape(1, 16),
-        band_widths.reshape(1, M),
+        *(
+            pltpu.with_memory_space_constraint(value, pltpu.HBM)
+            for value in (
+                ensemble,
+                innovation,
+                obs_weight,
+                lat_offset.reshape(1, 16),
+                lat_weight.reshape(1, 16),
+                band_widths.reshape(1, M),
+            )
+        )
     )
     return pl.pallas_call(
         finish,
@@ -551,16 +584,14 @@
             jax.ShapeDtypeStruct((2, 2), F32),
             jax.ShapeDtypeStruct((4, 8, M * LEV), BF16),
         ),
-        in_specs=[anywhere, anywhere],
+        in_specs=[in_vmem, in_vmem],
         out_specs=(anywhere, anywhere),
         scratch_shapes=[
-            vmem((8, 128), F32),
             vmem((2, 2), F32),
-            vmem((3, 4, 8, M * LEV), F32),
             vmem((4, 8, M * LEV), BF16),
-            dma((2, 5)),
+            dma((5,)),
         ],
-        compiler_params=pltpu.CompilerParams(vmem_limit_bytes=62 * 1024 * 1024),
+        compiler_params=pltpu.CompilerParams(vmem_limit_bytes=16 * 1024 * 1024),
         name="finish",
     )(table, u)
 

time: 58.8 us -> 55.8 us (0.949)
  Pallas kernels: 57.9 us -> 55.1 us
    pallas_call x1, Pallas kernels: 55.7 us -> 54.3 us  [per_device(): pl.pallas_call(functools.partial(kernel, topo, entries), out_shape=(jax.S...]
    pallas_call x1, Pallas kernels: 2.23 us -> 0.8 us  [per_device(): pl.pallas_call(finish, out_shape=(jax.ShapeDtypeStruct((2, 2), F32), jax....]
where the time goes in v2:
time: 55.8 us; the launch traced here: 55.7 us
  Pallas kernels  55.1 us (99%)
  between operations  0.64 us (1%)
    pallas_call x1, Pallas kernels, per_device(): pl.pallas_call(functools.partial(kernel, topo, entries), out_shape=(jax.S...  54.3 us

profile of v2, /device:TPU:2, one launch (start us, length us, event | category | flops | bytes accessed | tf_op | source)
XLA Modules:
  0.0 55.7 jit_solution(6483496537768874186)
XLA Ops:
  0.6 54.3 %lanczos.1 = (f32[8,128]{1,0:T(8,128)S(1)}, f32[3,4,8,5120]{3,2,1,0:T(8,128)S(1)}) custom-call(bf16[4,8,10240]{2,1,0:T(8,128)(2,1)} %ens_hbm.1, f32[8,16,128]{2,1,0:T(8,128)} %innov_hbm.1, f32[8,16,128]{2,1,0:T(8,128)} %wobs_hbm.1, s32[1,16]{1,0:T(1,128)} %bitcast.3, f32[1,16]{1,0:T(1,128)} %bitcast.4, s32[1,80]{1,0:T(1,128)} %bitcast.5), custom_call_target="tpu_custom_call" | custom-call | tf_op jit(solution)/shard_map/lanczos/pallas_call | solution.py:511
  54.9 0.8 %finish.1 = (f32[2,2]{1,0:T(2,128)}, bf16[4,8,5120]{2,1,0:T(8,128)(2,1)}) custom-call(f32[8,128]{1,0:T(8,128)S(1)} %get-tuple-element.4.table, f32[3,4,8,5120]{3,2,1,0:T(8,128)S(1)} %get-tuple-element.5.u), custom_call_target="tpu_custom_call" | custom-call | tf_op jit(solution)/shard_map/finish/pallas_call | solution.py:581

commit v3 on v2

--- a/solution.py
+++ b/solution.py
@@ -41,6 +41,7 @@
     hbuf,
     ybuf,
     yin,
+    wown,
     wext,
     wsplit,
     zext,
@@ -85,6 +86,9 @@
         else:
             pl.when((lat + dlat >= 0) & (lat + dlat < lat_n))(body)
 
+    def steps(count):
+        return sorted(range(1, count), key=lambda step: -min(step, count - step))
+
     def dev_a(i):
         return (z_hi * x_n + i // core_n, lon - core + i % core_n)
 
@@ -106,18 +110,19 @@
             ((bands_hbm, bands_ref), (weight_hbm, weight_ref), (offset_hbm, offset_ref))
         )
     ]
+    own_d = pltpu.make_async_copy(innov_hbm, down, local_sem.at[0])
+    own_w = pltpu.make_async_copy(wobs_hbm, wown, local_sem.at[1])
+    own_e = pltpu.make_async_copy(ens_hbm, ens, local_sem.at[2])
+    own_d.start()
+    own_w.start()
     for copy in small:
         copy.start()
-    own_d = pltpu.make_async_copy(innov_hbm, down, local_sem.at[0])
-    own_w = pltpu.make_async_copy(wobs_hbm, wext.at[3:11, 8:24], local_sem.at[1])
-    own_e = pltpu.make_async_copy(ens_hbm, ens, local_sem.at[2])
-
-    fown[...] = jnp.zeros(fown.shape, F32)
-    hbuf[...] = jnp.zeros(hbuf.shape, F32)
+
     yin[...] = jnp.zeros(yin.shape, F32)
     wext[...] = jnp.zeros(wext.shape, F32)
     zext[...] = jnp.zeros(zext.shape, F32)
     params[...] = jnp.zeros(params.shape, F32)
+
     barrier = pltpu.get_barrier_semaphore()
     for dlat, dlon in DIRECTIONS:
 
@@ -127,8 +132,8 @@
             )
 
         inside(dlat, greet)
-    for me, count, device, _, _, _ in stages:
-        for step in range(1, count):
+    for me, count, device, _, _, _ in reversed(stages):
+        for step in steps(count):
             pl.semaphore_signal(
                 barrier,
                 inc=1,
@@ -136,42 +141,18 @@
                 device_id_type=MESH,
             )
 
-    own_d.start()
-    own_w.start()
     own_e.start()
+    fown[...] = jnp.zeros(fown.shape, F32)
+    hbuf[...] = jnp.zeros(hbuf.shape, F32)
     for copy in small:
         copy.wait()
     params[1, 0:1, 0:16] = weight_ref[...]
     params[1, 1:2, 0:16] = offset_ref[...].astype(F32)
 
-    rows = lax.broadcasted_iota(jnp.int32, (128, 128), 0)
-    cols = lax.broadcasted_iota(jnp.int32, (128, 128), 1)
-    same = (rows < LEV) == (cols < LEV)
-    distance = jnp.where(same, jnp.abs(rows - cols), 1000)
-    first_half = lax.broadcasted_iota(jnp.int32, (1, 128), 1) < LEV
-
-    def build(j):
-        width = jnp.where(first_half, bands_ref[0, 2 * j] + 1, bands_ref[0, 2 * j + 1] + 1)
-        tent = jnp.maximum(width - distance, 0).astype(F32).astype(BF16)
-        wide = width.astype(F32)
-        scale = 1.0 / (wide * wide)
-        square = jnp.dot(tent, tent, preferred_element_type=F32) * (scale * scale)
-        high = square.astype(BF16)
-        tents[j] = tent
-        sq_hi[j] = high
-        sq_lo[j] = (square - high.astype(F32)).astype(BF16)
-        inv2[j] = jnp.broadcast_to(scale, (8, 128))
-
-    def build_some(step, carry):
-        for extra in range(UNROLL):
-            build(step * UNROLL + extra)
-        return carry
-
-    lax.fori_loop(0, PAIRS // UNROLL, build_some, 0)
-
     own_d.wait()
     own_w.wait()
-    fown[:, 8:24, :] = down[...] * wext[3:11, 8:24, :]
+    fown[:, 8:24, :] = down[...] * wown[...]
+    wext[3:11, 8:24, :] = wown[...]
 
     row = lax.broadcasted_iota(jnp.int32, (16, 128), 0)
     lane = lax.broadcasted_iota(jnp.int32, (16, 128), 1)
@@ -291,6 +272,31 @@
     for dlat, dlon in DIRECTIONS:
         inside(dlat, lambda dlat=dlat, dlon=dlon: weight_copy(dlat, dlon).start())
 
+    rows = lax.broadcasted_iota(jnp.int32, (128, 128), 0)
+    cols = lax.broadcasted_iota(jnp.int32, (128, 128), 1)
+    same = (rows < LEV) == (cols < LEV)
+    distance = jnp.where(same, jnp.abs(rows - cols), 1000)
+    first_half = lax.broadcasted_iota(jnp.int32, (1, 128), 1) < LEV
+
+    def build(j):
+        width = jnp.where(first_half, bands_ref[0, 2 * j] + 1, bands_ref[0, 2 * j + 1] + 1)
+        tent = jnp.maximum(width - distance, 0).astype(F32).astype(BF16)
+        wide = width.astype(F32)
+        scale = 1.0 / (wide * wide)
+        square = jnp.dot(tent, tent, preferred_element_type=F32) * (scale * scale)
+        high = square.astype(BF16)
+        tents[j] = tent
+        sq_hi[j] = high
+        sq_lo[j] = (square - high.astype(F32)).astype(BF16)
+        inv2[j] = jnp.broadcast_to(scale, (8, 128))
+
+    def build_some(step, carry):
+        for extra in range(UNROLL):
+            build(step * UNROLL + extra)
+        return carry
+
+    lax.fori_loop(0, PAIRS // UNROLL, build_some, 0)
+
     def restrict(fields):
         shares = [jnp.zeros((4, 16, 128), F32) for _ in range(5)]
         for parity in range(2):
@@ -422,11 +428,11 @@
             )
 
         slots[me] = local
-        for step in range(1, count):
+        for step in steps(count):
             stage_copy(lax.rem(me + step, count), me).start()
         if number == 0:
             spread(2)
-        for step in range(1, count):
+        for step in steps(count):
             other = lax.rem(me + step, count)
             stage_copy(other, other).wait_recv()
         local = slots[0]
@@ -438,18 +444,20 @@
         return jnp.broadcast_to(one, (8, 128))
 
     a, b, d, e, f = (picked(number) for number in range(5))
-    beta0 = jnp.sqrt(a / entries + EPSILON)
-    alpha0 = (a + b) / (entries * beta0 * beta0)
+    square0 = a * (1.0 / entries) + EPSILON
+    inverse0 = 1.0 / square0
+    alpha0 = (a + b) * (inverse0 * (1.0 / entries))
     rest = 1.0 - alpha0
-    square = (rest * rest * a + 2.0 * rest * b + d) / (beta0 * beta0)
-    beta1 = jnp.sqrt(square / entries + EPSILON)
-    mixed = (rest * rest * b + rest * (d + e) + f) / (beta0 * beta0)
-    alpha1 = (square + mixed) / (entries * beta1 * beta1)
-    back = ((rest * a + b) + (rest * b + e)) / (entries * beta0 * beta0 * beta1)
-    scale = 1.0 / (beta0 * beta1)
-    q2 = scale
-    q1 = (1.0 + rest - alpha1) * scale
-    q0 = (rest - alpha1 * rest) * scale - back / beta0
+    own1 = (rest * (rest * a) + 2.0 * (rest * b) + d) * inverse0
+    square1 = own1 * (1.0 / entries) + EPSILON
+    inverse1 = 1.0 / square1
+    mixed = (rest * (rest * b) + rest * (d + e) + f) * inverse0
+    alpha1 = (own1 + mixed) * (inverse1 * (1.0 / entries))
+    back = ((rest * a + b) + (rest * b + e)) * (inverse0 * (1.0 / entries))
+    beta0, beta1 = jnp.sqrt(square0), jnp.sqrt(square1)
+    q2 = jnp.sqrt(inverse0 * inverse1)
+    q1 = (1.0 + rest - alpha1) * q2
+    q0 = (rest - alpha1 * rest - back) * q2
     row8 = lax.broadcasted_iota(jnp.int32, (8, 128), 0)
     left = lax.broadcasted_iota(jnp.int32, (8, 128), 1) == 0
     table = jnp.where(row8 == 0, jnp.where(left, alpha0, alpha1), jnp.where(left, beta0, beta1))
@@ -469,7 +477,7 @@
 
         inside(dlat, drain)
     for me, count, device, slots, send_sems, recv_sems in stages:
-        for step in range(1, count):
+        for step in steps(count):
             target = lax.rem(me + step, count)
             pltpu.make_async_remote_copy(
                 src_ref=slots.at[me],
@@ -533,6 +541,7 @@
             vmem((5, 8, 32, 128), F32),
             vmem((8, 24, 128), F32),
             vmem((8, 4, 8, 128), F32),
+            vmem((8, 16, 128), F32),
             vmem((14, 40, 128), F32),
             vmem((2, 2, 7, 16, 128), F32),
             vmem((2, 10, 24, 128), F32),

time: 55.8 us -> 55.2 us (0.989)
  Pallas kernels: 55.1 us -> 54.4 us
    pallas_call x1, Pallas kernels: 54.3 us -> 53.6 us  [per_device(): pl.pallas_call(functools.partial(kernel, topo, entries), out_shape=(jax.S...]
where the time goes in v3:
time: 55.2 us; the launch traced here: 55.1 us
  Pallas kernels  54.4 us (99%)
  between operations  0.64 us (1%)
    pallas_call x1, Pallas kernels, per_device(): pl.pallas_call(functools.partial(kernel, topo, entries), out_shape=(jax.S...  53.6 us

profile of v3, /device:TPU:2, one launch (start us, length us, event | category | flops | bytes accessed | tf_op | source)
XLA Modules:
  0.0 55.1 jit_solution(3116920254863577803)
XLA Ops:
  0.6 53.6 %lanczos.1 = (f32[8,128]{1,0:T(8,128)S(1)}, f32[3,4,8,5120]{3,2,1,0:T(8,128)S(1)}) custom-call(bf16[4,8,10240]{2,1,0:T(8,128)(2,1)} %ens_hbm.1, f32[8,16,128]{2,1,0:T(8,128)} %innov_hbm.1, f32[8,16,128]{2,1,0:T(8,128)} %wobs_hbm.1, s32[1,16]{1,0:T(1,128)} %bitcast.3, f32[1,16]{1,0:T(1,128)} %bitcast.4, s32[1,80]{1,0:T(1,128)} %bitcast.5), custom_call_target="tpu_custom_call" | custom-call | tf_op jit(solution)/shard_map/lanczos/pallas_call | solution.py:519
  54.3 0.8 %finish.1 = (f32[2,2]{1,0:T(2,128)}, bf16[4,8,5120]{2,1,0:T(8,128)(2,1)}) custom-call(f32[8,128]{1,0:T(8,128)S(1)} %get-tuple-element.4.table, f32[3,4,8,5120]{3,2,1,0:T(8,128)S(1)} %get-tuple-element.5.u), custom_call_target="tpu_custom_call" | custom-call | tf_op jit(solution)/shard_map/finish/pallas_call | solution.py:590
